TPU v7x, 128 devices: a whole 4x4x4 slice. The times are simulated.
128 devices in a mesh: grp: 16 (over z, x), reg: 8 (over y, core).
Axes of the slice: x: 4, y: 4, z: 4, core: 2. Of those that a mesh axis runs over, the one named last changes fastest.
Arguments:
- orbitals: bfloat16 [8, 16, 512, 1024], P('reg', 'grp'), may hold values from -6 to 6
- occupied: bfloat16 [8, 16, 8, 512], P('reg', 'grp'), may hold values from -0.59765625 to 0.59765625
- panel_index: int32 [128], replicated, may hold values from 0 to 1023, as said below
- screening: bfloat16 [896, 512, 512], P(('grp', 'reg')), may hold values from -0.25 to 0.25
- block_region: int32 [896, 1], P(('grp', 'reg')), may hold values from 0 to 7; in each aligned block of 7 rows (0 to 6, 7 to 13, ...) at most 2 rows name the same one
- block_row: int32 [896], P(('grp', 'reg')), may hold values from 0 to 15
- block_col: int32 [896], P(('grp', 'reg')), may hold values from 0 to 15
Outputs:
- sigma: float32 [8, 128, 128], P('reg')
Inputs may be any that keep to these rules, and one draw needn't show every extreme that they name: `panel_index`: the 128 indices are distinct. Among the 7 blocks of one device (aligned rows of block_region), at most 2 name the same region.
All inputs are finite; a program needn't handle non-finite values.
Results may differ from a plain program's by a relative error of at most 0.0054.
Values may be sent and summed in bfloat16 or wider, within the bound.
A program may use at most 192 MiB of HBM per device.

v0:
```python
import jax
import jax.numpy as jnp
from jax import lax
from jax.sharding import PartitionSpec as P

CAP = 2


def form_pairs(orbital_rows, occupied_rows):
    pairs = orbital_rows[..., :, None, :].astype(jnp.float32) * jnp.swapaxes(occupied_rows, -1, -2)[
        ..., None
    ].astype(jnp.float32)
    return pairs.astype(jnp.bfloat16)


def shards(orbitals, occupied, panel_index, screening, block_region, block_row, block_col):
    regions = lax.axis_size("reg")
    panel_orbs = jnp.take(orbitals[0], panel_index, axis=2)
    occ_rows = occupied[0]
    grid_points = screening.shape[1]
    panel_width = panel_orbs.shape[2]
    occ_count = occ_rows.shape[1]
    held_count = screening.shape[0]
    slot_count = regions * CAP
    destination = block_region[:, 0]
    membership = (destination[:, None] == jnp.arange(regions, dtype=jnp.int32)[None, :]).astype(
        jnp.int32
    )
    earlier = jnp.cumsum(membership, axis=0) - membership
    slot_of = destination * CAP + jnp.sum(earlier * membership, axis=1)
    matched = (slot_of[None, :] == jnp.arange(slot_count, dtype=jnp.int32)[:, None]).astype(
        jnp.int32
    )
    filled = jnp.sum(matched, axis=1)
    source = jnp.sum(matched * jnp.arange(held_count, dtype=jnp.int32)[None, :], axis=1)
    outgoing = jnp.take(screening, source, axis=0) * filled[:, None, None].astype(jnp.bfloat16)
    labels = jnp.stack(
        [jnp.take(block_row, source) * filled, jnp.take(block_col, source) * filled, filled], axis=1
    )
    gathered = lax.all_gather(form_pairs(panel_orbs, occ_rows), "grp", axis=0, tiled=True)

    def select_pairs(indices):
        return jnp.take(gathered, indices, axis=0)

    incoming, arrived = (
        lax.all_to_all(
            outgoing.reshape(regions, CAP, grid_points, grid_points),
            "reg",
            split_axis=0,
            concat_axis=0,
            tiled=True,
        ),
        lax.all_to_all(
            labels.reshape(regions, CAP, 3), "reg", split_axis=0, concat_axis=0, tiled=True
        ),
    )
    incoming = incoming.reshape(slot_count, grid_points, grid_points)
    arrived = arrived.reshape(slot_count, 3)
    col_pairs = select_pairs(arrived[:, 1]).reshape(
        slot_count, grid_points, occ_count * panel_width
    )
    screened = jnp.einsum(
        "spq,sqc->spc", incoming, col_pairs, preferred_element_type=jnp.float32
    ).astype(jnp.bfloat16)
    row_pairs = select_pairs(arrived[:, 0]).reshape(
        slot_count, grid_points * occ_count, panel_width
    )
    partial_sigma = jnp.einsum(
        "sri,srj->ij",
        row_pairs,
        screened.reshape(slot_count, grid_points * occ_count, panel_width),
        preferred_element_type=jnp.float32,
    )
    sigma = lax.psum(partial_sigma, "grp")
    return sigma[None]


def solution(mesh):
    in_specs = (
        P("reg", "grp", None, None),
        P("reg", "grp", None, None),
        P(),
        P(("grp", "reg"), None, None),
        P(("grp", "reg"), None),
        P(("grp", "reg")),
        P(("grp", "reg")),
    )
    out_specs = P("reg", None, None)
    return jax.shard_map(shards, mesh=mesh, in_specs=in_specs, out_specs=out_specs, check_vma=False)
```

profile of v0, /device:TPU:0, one launch (start us, length us, event | category | flops | bytes accessed | tf_op | source)
XLA Modules:
  0.0 339.5 jit_solution(4951172310689396512)
XLA Ops:
  6.5 0.0 copy-start
  6.5 0.0 all-gather.2.cloned.1.call-start
  6.5 0.7 compare_and_fusion.4
  7.2 0.7 compare_select_fusion.5
  7.9 0.7 convert_bitcast_fusion.1
  8.6 0.1 copy.28
  8.7 1.5 copy.26
  10.2 0.8 gather_fusion
  11.1 0.1 convert_bitcast_fusion
  11.2 0.1 copy.27
  11.3 1.6 multiply_convert_fusion
  12.9 0.0 all-gather.2.cloned.1.call-update
  12.9 0.7 fusion.8
  13.6 0.8 select_reduce_fusion.1
  14.5 0.7 multiply_add_fusion
  15.1 0.1 convert_reduce_fusion
  15.2 0.0 copy-done
  15.2 0.7 gather_fusion.3
  15.9 1.3 gather_fusion.2
  17.2 0.1 stack.14
  17.3 0.1 stack.12
  17.4 0.1 stack.13
  17.5 0.7 copy.24
  18.2 4.6 %all-to-all-start = ((s32[8,2,3]{2,1,0:T(2,128)}), s32[8,2,3]{2,1,0:T(2,128)S(1)}, u32[]{:S(2)}, u32[]{:S(2)}) async-start(s32[8,2,3]{2,1,0:T(2,128)} %copy.24), calls=%async_computation | async-start | bytes 16384 | tf_op jit(solution)/shard_map/all_to_all | solution.py:53
  22.8 0.1 reduce_sum.34
  22.9 0.1 convert_element_type.65
  23.0 6.9 %gather_fusion.1 = bf16[16,512,512]{2,1,0:T(8,128)(2,1)} fusion(bf16[7,512,512]{2,1,0:T(8,128)(2,1)} %param.14, s32[1024]{0:T(1024)S(1)} %pad_clamp_fusion.1), kind=kCustom, calls=%fused_computation.5 | custom fusion | bytes 16777280 | tf_op jit(solution)/shard_map/jit(_take)/gather | solution.py:36
  29.9 7.4 %select_multiply_fusion = bf16[8,2,512,512]{3,2,1,0:T(8,128)(2,1)} fusion(bf16[8,2,512,512]{3,2,1,0:T(8,128)(2,1)} %bitcast.40, pred[8,2]{1,0:T(8,128)(4,1)S(1)} %compare_and_fusion, bf16[8,2]{1,0:T(8,128)(2,1)S(1)} %convert_element_type.65), kind=kLoop, calls=%fused_computation.13 | loop fusion | flops 8388608 | bytes 16777264 | tf_op jit(solution)/shard_map/mul | solution.py:36
  37.4 0.0 all-to-all-done
  37.4 5.0 %all-to-all-start.1 = ((bf16[8,2,512,512]{3,2,1,0:T(8,128)(2,1)}), bf16[8,2,512,512]{3,2,1,0:T(8,128)(2,1)}, u32[]{:S(2)}, u32[]{:S(2)}) async-start(bf16[8,2,512,512]{3,2,1,0:T(8,128)(2,1)} %select_multiply_fusion), calls=%async_computation.1 | async-start | bytes 16777216 | tf_op jit(solution)/shard_map/all_to_all | solution.py:46
  42.3 0.2 all-reduce.2.cloned.1.call-start
  42.6 0.1 fusion.11
  42.6 0.1 copy.32
  42.7 0.1 copy.33
  42.9 84.2 %all-gather.2.cloned.1.call-done = bf16[16,512,8,128]{3,2,1,0:T(8,128)(2,1)} async-done(((bf16[1,512,8,128]{3,2,1,0:T(8,128)(2,1)}), bf16[16,512,8,128]{3,2,1,0:T(8,128)(2,1)}) %all-gather.2.cloned.1.call-update) | async-done | bytes 16777232 | tf_op jit(solution)/shard_map/all_gather | solution.py:40
  127.0 13.0 %gather_fusion.5 = bf16[16,512,8,128]{3,2,1,0:T(8,128)(2,1)} fusion(bf16[16,512,8,128]{3,2,1,0:T(8,128)(2,1)} %all-gather.2.cloned.1.call-done, s32[1024]{0:T(1024)S(1)} %pad_clamp_fusion), kind=kCustom, calls=%fused_computation.3.clone | custom fusion | bytes 33554496 | tf_op jit(solution)/shard_map/jit(_take)/gather | solution.py:43
  140.0 14.2 %broadcast_select_fusion = bf16[16,512,8,128]{3,2,1,0:T(8,128)(2,1)} fusion(bf16[16,512,8,128]{3,2,1,0:T(8,128)(2,1)} %gather_fusion.5, pred[16]{0:T(512)(128)(4,1)S(1)} %compare_and_fusion.1), kind=kLoop, calls=%fused_computation.9 | loop fusion | flops 8388608 | bytes 33554448 | tf_op jit(solution)/shard_map/jit(_take)/select_n | solution.py:43
  154.2 25.3 %reshape.130 = bf16[16,512,1024]{2,1,0:T(8,128)(2,1)} reshape(bf16[16,512,8,128]{3,2,1,0:T(8,128)(2,1)} %broadcast_select_fusion) | data formatting | bytes 33554432 | tf_op jit(solution)/shard_map/reshape | solution.py:59
  179.5 0.0 all-to-all-done.1
  179.5 17.0 %convolution_convert_fusion = bf16[16,512,1024]{2,1,0:T(8,128)(2,1)} fusion(bf16[16,512,512]{2,1,0:T(8,128)(2,1)} %bitcast.12, bf16[16,512,1024]{2,1,0:T(8,128)(2,1)} %reshape.130), kind=kOutput, calls=%fused_computation.11 | convolution fusion | flops 8598323200 | bytes 41943040 | tf_op jit(solution)/shard_map/spq,sqc->spc/dot_general | solution.py:62
  196.4 25.3 %reshape.131 = bf16[16,4096,128]{2,1,0:T(8,128)(2,1)} reshape(bf16[16,512,1024]{2,1,0:T(8,128)(2,1)} %convolution_convert_fusion) | data formatting | bytes 33554432 | tf_op jit(solution)/shard_map/reshape | solution.py:71
  221.7 0.0 copy-start.1
  221.7 13.0 %gather_fusion.4 = bf16[16,512,8,128]{3,2,1,0:T(8,128)(2,1)} fusion(bf16[16,512,8,128]{3,2,1,0:T(8,128)(2,1)} %all-gather.2.cloned.1.call-done, s32[1024]{0:T(1024)S(1)} %pad_clamp_fusion.2), kind=kCustom, calls=%fused_computation.1.clone | custom fusion | bytes 33554496 | tf_op jit(solution)/shard_map/jit(_take)/gather | solution.py:43
  234.7 16.3 %fusion.5 = f32[1,128,128]{2,1,0:T(8,128)} fusion(bf16[16,4096,128]{2,1,0:T(8,128)(2,1)} %reshape.131, bf16[16,512,8,128]{3,2,1,0:T(8,128)(2,1)} %gather_fusion.4, pred[16]{0:T(512)(128)(4,1)S(1)} %compare_and_fusion.2), kind=kOutput, calls=%fused_computation.15 | convolution fusion | flops 2155872256 | bytes 33619984 | tf_op jit(solution)/shard_map/sri,srj->ij/dot_general | solution.py:68
  251.0 0.0 all-reduce.2.cloned.1.call-update
  251.0 80.2 %all-reduce.2.cloned.1.call-done = f32[1,128,128]{2,1,0:T(8,128)} async-done(((f32[1,128,128]{2,1,0:T(8,128)}), f32[1,128,128]{2,1,0:T(8,128)}) %all-reduce.2.cloned.1.call-update) | async-done | bytes 65552 | tf_op jit(solution)/shard_map/psum | solution.py:74
  331.2 1.5 copy.35
  332.7 0.0 copy-done.1
  (15 shorter events, 0.1 us)
Async XLA Ops:
  6.5 8.7 %copy-start = (s32[7]{0:T(128)S(1)}, s32[7]{0:T(128)}, u32[]{:S(2)}) copy-start(s32[7]{0:T(128)} %param.17) | copy-start | bytes 88
  6.5 120.5 %all-gather.2.cloned.1.call-start = ((), (), s32[]{:S(2)}) async-start(), calls=%async_computation.2 | async-start | bytes 17825792 | tf_op jit(solution)/shard_map/all_gather | solution.py:40
  18.2 19.1 %all-to-all-start = ((s32[8,2,3]{2,1,0:T(2,128)}), s32[8,2,3]{2,1,0:T(2,128)S(1)}, u32[]{:S(2)}, u32[]{:S(2)}) async-start(s32[8,2,3]{2,1,0:T(2,128)} %copy.24), calls=%async_computation | async-start | bytes 16384 | tf_op jit(solution)/shard_map/all_to_all | solution.py:53
  37.4 142.1 %all-to-all-start.1 = ((bf16[8,2,512,512]{3,2,1,0:T(8,128)(2,1)}), bf16[8,2,512,512]{3,2,1,0:T(8,128)(2,1)}, u32[]{:S(2)}, u32[]{:S(2)}) async-start(bf16[8,2,512,512]{3,2,1,0:T(8,128)(2,1)} %select_multiply_fusion), calls=%async_computation.1 | async-start | bytes 16777216 | tf_op jit(solution)/shard_map/all_to_all | solution.py:46
  42.3 288.9 %all-reduce.2.cloned.1.call-start = ((), (), s32[]{:S(2)}) async-start(), calls=%async_computation.3 | async-start | bytes 131072 | tf_op jit(solution)/shard_map/psum | solution.py:74
  221.7 111.0 %copy-start.1 = (s32[7]{0:T(128)S(1)}, s32[7]{0:T(128)}, u32[]{:S(2)}) copy-start(s32[7]{0:T(128)} %param.17) | copy-start | bytes 88
Sparse Core Ops, SparseCore 0:
  13.0 113.9 all-gather.1
  251.1 80.0 all-reduce.1
where the time goes:
time: 341 us; the launch traced here: 340 us
  waiting for transfers between devices  164 us (48%)
  local copies, waits for them, and re-layouts  90.9 us (27%)
  matrix products  33.3 us (10%)
  other arithmetic  27.7 us (8%)
  between operations  13.5 us (4%)
  starting transfers between devices  9.74 us (3%)
    all_gather x1, waiting for transfers between devices, shards(): lax.all_gather(form_pairs(panel_orbs, occ_rows), 'grp', axis=0, tiled=True)  84.2 us
    psum x1, waiting for transfers between devices, shards(): sigma = lax.psum(partial_sigma, 'grp')  80.2 us
    gather x2, local copies, waits for them, and re-layouts, select_pairs(): return jnp.take(gathered, indices, axis=0)  25.9 us
    reshape x1, local copies, waits for them, and re-layouts, shards(): select_pairs(arrived[:, 1])  25.3 us
    reshape x1, local copies, waits for them, and re-layouts, shards(): screened.reshape(slot_count, grid_points * occ_count, panel_width)  25.3 us
    dot_general x1, matrix products, shards(): jnp.einsum('spq,sqc->spc', incoming, col_pairs, preferred_element_type=jn...  17 us
    dot_general x1, matrix products, shards(): jnp.einsum('sri,srj->ij', row_pairs, screened.reshape(slot_count, grid_po...  16.3 us
    select_n x3, other arithmetic, select_pairs(): return jnp.take(gathered, indices, axis=0)  14.2 us
  transfers between devices with their start and end apart: 4, of which 2 were waited for; matrix products, arithmetic and copies ran while one was open for 21% of the time, Pallas kernels for 0%

commit v1 on v0

--- a/solution.py
+++ b/solution.py
@@ -37,7 +37,11 @@
     labels = jnp.stack(
         [jnp.take(block_row, source) * filled, jnp.take(block_col, source) * filled, filled], axis=1
     )
-    gathered = lax.all_gather(form_pairs(panel_orbs, occ_rows), "grp", axis=0, tiled=True)
+    block = form_pairs(panel_orbs, occ_rows)
+    size = lax.axis_size("grp")
+    blocks = jnp.stack([block for _ in range(size)])
+    blocks = lax.all_to_all(blocks, "grp", split_axis=0, concat_axis=0)
+    gathered = jnp.concatenate(blocks, axis=0)
 
     def select_pairs(indices):
         return jnp.take(gathered, indices, axis=0)

time: 341 us -> 534 us (1.57)
  waiting for transfers between devices: 164 us -> 344 us
  starting transfers between devices: 9.74 us -> 17.7 us
  local copies, waits for them, and re-layouts: 90.9 us -> 96.7 us
    all_to_all x0 -> x1, waiting for transfers between devices: none -> 239 us  [shards(): blocks = lax.all_to_all(blocks, 'grp', split_axis=0, concat_axis=0)]
    all_gather x1 -> x0, waiting for transfers between devices: 84.2 us -> none  [shards(): lax.all_gather(form_pairs(panel_orbs, occ_rows), 'grp', axis=0, tiled=True)]
    all_to_all x1, waiting for transfers between devices: 0.01 us -> 28.7 us  [shards(): lax.all_to_all(outgoing.reshape(regions, CAP, grid_points, grid_points),...]
    all_to_all x0 -> x1, starting transfers between devices: none -> 7.93 us  [shards(): blocks = lax.all_to_all(blocks, 'grp', split_axis=0, concat_axis=0)]
    another operation x0 -> x1, local copies, waits for them, and re-layouts: none -> 6.14 us  [shards(): blocks = jnp.stack([block for _ in range(size)])]
  transfers between devices with their start and end apart: 4 -> 4, of which waited for: 2 -> 3; matrix products, arithmetic and copies ran while one was open for 21% -> 16% of each run, Pallas kernels for 0% -> 0%
where the time goes in v1:
time: 534 us; the launch traced here: 532 us
  waiting for transfers between devices  344 us (64%)
  local copies, waits for them, and re-layouts  96.7 us (18%)
  matrix products  33.2 us (6%)
  other arithmetic  26.8 us (5%)
  starting transfers between devices  17.7 us (3%)
  between operations  13.5 us (3%)
    all_to_all x1, waiting for transfers between devices, shards(): blocks = lax.all_to_all(blocks, 'grp', split_axis=0, concat_axis=0)  239 us
    psum x1, waiting for transfers between devices, shards(): sigma = lax.psum(partial_sigma, 'grp')  76 us
    all_to_all x1, waiting for transfers between devices, shards(): lax.all_to_all(outgoing.reshape(regions, CAP, grid_points, grid_points),...  28.7 us
    gather x2, local copies, waits for them, and re-layouts, select_pairs(): return jnp.take(gathered, indices, axis=0)  25.9 us
    reshape x1, local copies, waits for them, and re-layouts, shards(): screened.reshape(slot_count, grid_points * occ_count, panel_width)  25.3 us
    reshape x1, local copies, waits for them, and re-layouts, shards(): select_pairs(arrived[:, 1])  25.3 us
    dot_general x1, matrix products, shards(): jnp.einsum('spq,sqc->spc', incoming, col_pairs, preferred_element_type=jn...  16.9 us
    dot_general x1, matrix products, shards(): jnp.einsum('sri,srj->ij', row_pairs, screened.reshape(slot_count, grid_po...  16.3 us
  transfers between devices with their start and end apart: 4, of which 3 were waited for; matrix products, arithmetic and copies ran while one was open for 16% of the time, Pallas kernels for 0%

profile of v1, /device:TPU:0, one launch (start us, length us, event | category | flops | bytes accessed | tf_op | source)
XLA Modules:
  0.0 531.7 jit_solution(8971619921990577692)
XLA Ops:
  6.5 0.0 copy-start
  6.5 0.7 fusion.8
  7.3 0.8 select_reduce_fusion.1
  8.1 0.7 multiply_add_fusion
  8.8 0.1 convert_reduce_fusion
  8.9 0.0 copy-done
  8.9 0.7 gather_fusion.3
  9.6 1.3 gather_fusion.2
  10.9 0.1 stack.13
  11.0 0.1 stack.11
  11.1 0.1 stack.12
  11.2 0.7 copy.24
  11.9 4.6 all-to-all-start.1
  16.4 0.7 compare_and_fusion.4
  17.1 0.7 compare_select_fusion.5
  17.8 0.7 convert_bitcast_fusion.1
  18.5 0.1 copy.28
  18.6 1.5 copy.26
  20.1 0.8 gather_fusion
  21.0 0.1 convert_bitcast_fusion
  21.1 0.1 copy.27
  21.2 0.7 multiply_convert_fusion
  21.9 0.0 all-to-all-done.1
  21.9 6.1 %stack.10 = bf16[16,1,512,8,128]{4,3,2,1,0:T(8,128)(2,1)} broadcast(bf16[512,8,128]{2,1,0:T(8,128)(2,1)S(1)} %multiply_convert_fusion), dimensions={2,3,4} | broadcast | bytes 17825792 | tf_op jit(solution)/shard_map/stack | solution.py:42
  28.1 7.9 %all-to-all-start = ((bf16[16,1,512,8,128]{4,3,2,1,0:T(8,128)(2,1)}), bf16[16,1,512,8,128]{4,3,2,1,0:T(8,128)(2,1)}, u32[]{:S(2)}, u32[]{:S(2)}) async-start(bf16[16,1,512,8,128]{4,3,2,1,0:T(8,128)(2,1)} %stack.10), calls=%async_computation | async-start | bytes 33554432 | tf_op jit(solution)/shard_map/all_to_all | solution.py:43
  36.0 0.1 reduce_sum.34
  36.1 0.1 convert_element_type.64
  36.2 6.7 %gather_fusion.1 = bf16[16,512,512]{2,1,0:T(8,128)(2,1)} fusion(bf16[7,512,512]{2,1,0:T(8,128)(2,1)} %param.14, s32[1024]{0:T(1024)S(1)} %pad_clamp_fusion.1), kind=kCustom, calls=%fused_computation.5 | custom fusion | bytes 16777280 | tf_op jit(solution)/shard_map/jit(_take)/gather | solution.py:36
  42.9 7.4 %select_multiply_fusion = bf16[8,2,512,512]{3,2,1,0:T(8,128)(2,1)} fusion(bf16[8,2,512,512]{3,2,1,0:T(8,128)(2,1)} %bitcast.41, pred[8,2]{1,0:T(8,128)(4,1)S(1)} %compare_and_fusion, bf16[8,2]{1,0:T(8,128)(2,1)S(1)} %convert_element_type.64), kind=kLoop, calls=%fused_computation.13 | loop fusion | flops 8388608 | bytes 16777264 | tf_op jit(solution)/shard_map/mul | solution.py:36
  50.3 238.9 %all-to-all-done = bf16[16,1,512,8,128]{4,3,2,1,0:T(8,128)(2,1)} async-done(((bf16[16,1,512,8,128]{4,3,2,1,0:T(8,128)(2,1)}), bf16[16,1,512,8,128]{4,3,2,1,0:T(8,128)(2,1)}, u32[]{:S(2)}, u32[]{:S(2)}) %all-to-all-start) | async-done | bytes 16777248 | tf_op jit(solution)/shard_map/all_to_all | solution.py:43
  289.2 5.0 all-to-all-start.2
  294.2 0.2 all-reduce.2.cloned.1.call-start
  294.4 0.1 fusion.11
  294.5 0.1 copy.32
  294.5 0.1 copy.33
  294.7 13.0 %gather_fusion.5 = bf16[16,512,8,128]{3,2,1,0:T(8,128)(2,1)} fusion(bf16[16,512,8,128]{3,2,1,0:T(8,128)(2,1)} %bitcast.8, s32[1024]{0:T(1024)S(1)} %pad_clamp_fusion), kind=kCustom, calls=%fused_computation.3.clone | custom fusion | bytes 33554496 | tf_op jit(solution)/shard_map/jit(_take)/gather | solution.py:47
  307.6 12.9 %gather_fusion.4 = bf16[16,512,8,128]{3,2,1,0:T(8,128)(2,1)} fusion(bf16[16,512,8,128]{3,2,1,0:T(8,128)(2,1)} %bitcast.8, s32[1024]{0:T(1024)S(1)} %pad_clamp_fusion.2), kind=kCustom, calls=%fused_computation.1.clone | custom fusion | bytes 33554496 | tf_op jit(solution)/shard_map/jit(_take)/gather | solution.py:47
  320.6 14.2 %broadcast_select_fusion = bf16[16,512,8,128]{3,2,1,0:T(8,128)(2,1)} fusion(bf16[16,512,8,128]{3,2,1,0:T(8,128)(2,1)} %gather_fusion.5, pred[16]{0:T(512)(128)(4,1)S(1)} %compare_and_fusion.1), kind=kLoop, calls=%fused_computation.9 | loop fusion | flops 8388608 | bytes 33554448 | tf_op jit(solution)/shard_map/jit(_take)/select_n | solution.py:47
  334.7 25.3 %reshape.132 = bf16[16,512,1024]{2,1,0:T(8,128)(2,1)} reshape(bf16[16,512,8,128]{3,2,1,0:T(8,128)(2,1)} %broadcast_select_fusion) | data formatting | bytes 33554432 | tf_op jit(solution)/shard_map/reshape | solution.py:63
  360.0 28.7 %all-to-all-done.2 = bf16[8,2,512,512]{3,2,1,0:T(8,128)(2,1)} async-done(((bf16[8,2,512,512]{3,2,1,0:T(8,128)(2,1)}), bf16[8,2,512,512]{3,2,1,0:T(8,128)(2,1)}, u32[]{:S(2)}, u32[]{:S(2)}) %all-to-all-start.2) | async-done | bytes 8388640 | tf_op jit(solution)/shard_map/all_to_all | solution.py:50
  388.8 16.9 %convolution_convert_fusion = bf16[16,512,1024]{2,1,0:T(8,128)(2,1)} fusion(bf16[16,512,512]{2,1,0:T(8,128)(2,1)} %bitcast.13, bf16[16,512,1024]{2,1,0:T(8,128)(2,1)} %reshape.132), kind=kOutput, calls=%fused_computation.11 | convolution fusion | flops 8598323200 | bytes 41943040 | tf_op jit(solution)/shard_map/spq,sqc->spc/dot_general | solution.py:66
  405.7 0.0 copy-start.1
  405.7 25.3 %reshape.133 = bf16[16,4096,128]{2,1,0:T(8,128)(2,1)} reshape(bf16[16,512,1024]{2,1,0:T(8,128)(2,1)} %convolution_convert_fusion) | data formatting | bytes 33554432 | tf_op jit(solution)/shard_map/reshape | solution.py:75
  431.0 16.3 %fusion.5 = f32[1,128,128]{2,1,0:T(8,128)} fusion(bf16[16,4096,128]{2,1,0:T(8,128)(2,1)} %reshape.133, bf16[16,512,8,128]{3,2,1,0:T(8,128)(2,1)} %gather_fusion.4, pred[16]{0:T(512)(128)(4,1)S(1)} %compare_and_fusion.2), kind=kOutput, calls=%fused_computation.15 | convolution fusion | flops 2155872256 | bytes 33619984 | tf_op jit(solution)/shard_map/sri,srj->ij/dot_general | solution.py:72
  447.3 0.0 all-reduce.2.cloned.1.call-update
  447.4 76.0 %all-reduce.2.cloned.1.call-done = f32[1,128,128]{2,1,0:T(8,128)} async-done(((f32[1,128,128]{2,1,0:T(8,128)}), f32[1,128,128]{2,1,0:T(8,128)}) %all-reduce.2.cloned.1.call-update) | async-done | bytes 65552 | tf_op jit(solution)/shard_map/psum | solution.py:78
  523.3 1.5 copy.35
  524.8 0.0 copy-done.1
  (15 shorter events, 0.1 us)
Async XLA Ops:
  6.5 2.4 copy-start
  11.9 10.0 %all-to-all-start.1 = ((s32[8,2,3]{2,1,0:T(2,128)}), s32[8,2,3]{2,1,0:T(2,128)S(1)}, u32[]{:S(2)}, u32[]{:S(2)}) async-start(s32[8,2,3]{2,1,0:T(2,128)} %copy.24), calls=%async_computation.1 | async-start | bytes 16384 | tf_op jit(solution)/shard_map/all_to_all | solution.py:57
  28.1 261.1 %all-to-all-start = ((bf16[16,1,512,8,128]{4,3,2,1,0:T(8,128)(2,1)}), bf16[16,1,512,8,128]{4,3,2,1,0:T(8,128)(2,1)}, u32[]{:S(2)}, u32[]{:S(2)}) async-start(bf16[16,1,512,8,128]{4,3,2,1,0:T(8,128)(2,1)} %stack.10), calls=%async_computation | async-start | bytes 33554432 | tf_op jit(solution)/shard_map/all_to_all | solution.py:43
  289.2 99.6 %all-to-all-start.2 = ((bf16[8,2,512,512]{3,2,1,0:T(8,128)(2,1)}), bf16[8,2,512,512]{3,2,1,0:T(8,128)(2,1)}, u32[]{:S(2)}, u32[]{:S(2)}) async-start(bf16[8,2,512,512]{3,2,1,0:T(8,128)(2,1)} %select_multiply_fusion), calls=%async_computation.2 | async-start | bytes 16777216 | tf_op jit(solution)/shard_map/all_to_all | solution.py:50
  294.2 229.2 %all-reduce.2.cloned.1.call-start = ((), (), s32[]{:S(2)}) async-start(), calls=%async_computation.3 | async-start | bytes 131072 | tf_op jit(solution)/shard_map/psum | solution.py:78
  405.7 119.1 %copy-start.1 = (s32[7]{0:T(128)S(1)}, s32[7]{0:T(128)}, u32[]{:S(2)}) copy-start(s32[7]{0:T(128)} %param.17) | copy-start | bytes 88
Sparse Core Ops, SparseCore 0:
  447.5 75.8 all-reduce.1
